TPU v7x, 1024 devices: a whole 4x8x16 slice. The times are simulated.
1024 devices in a mesh: row: 32 (over z_lo, y), col: 32 (over x, z_hi, core).
Axes of the slice: x: 4, y: 8, z: 16 (z_hi: 4, z_lo: 4; z = z_hi * 4 + z_lo), core: 2. Of those that a mesh axis runs over, the one named last changes fastest.
Arguments:
- coeff: bfloat16 [12288, 12288], P('row', 'col'), may hold values from -6 to 6
- bank: bfloat16 [16, 384, 384], replicated, may hold values from -0.09375 to 0.09375
- alpha_tiles: int32 [32, 24], replicated, may hold values from 0 to 31
- alpha_blocks: int32 [32, 24], replicated, may hold values from 0 to 15
- alpha_count: int32 [32], replicated, may hold values from 2 to 24, as said below
- beta_tiles: int32 [32, 24], replicated, may hold values from 0 to 31
- beta_blocks: int32 [32, 24], replicated, may hold values from 0 to 15
- beta_count: int32 [32], replicated, may hold values from 2 to 24, as said below
Outputs:
- sigma: float32 [12288, 12288], P('row', 'col')
Inputs may be any that keep to these rules, and one draw needn't show every extreme that they name: `alpha_count`: every value lies in 2 to 24; some tile has all 24 slots live. `beta_count`: every value lies in 2 to 24; some tile has all 24 slots live.
All inputs are finite; a program needn't handle non-finite values.
Results may differ from a plain program's by a relative error of at most 0.0003.
Values may be sent and summed in bfloat16 or wider, within the bound.
No kernel may reach another device: no remote copies, remote signals or barrier semaphores. Data moves between devices by JAX's collectives and lax.ppermute only.
A program may use at most 64 MiB of HBM per device.

v0:
```python
import jax
import jax.numpy as jnp
from jax import lax
from jax.experimental import pallas as pl
from jax.experimental.pallas import tpu as pltpu
from jax.sharding import PartitionSpec as P

LANE = 128
PAD = 16
FOOT = 2
PAIR = 2
CHAINS = 2
ROOM = 24 << 20
VMEM = pl.BlockSpec(memory_space=pltpu.VMEM)
SMEM = pl.BlockSpec(memory_space=pltpu.SMEM)


def inside(x):
    return pltpu.with_memory_space_constraint(x, pltpu.VMEM)


def blocks_of(width, tile):
    return width * tile // LANE


def ship(flat, parts, axis, fold):
    rows = flat.shape[0] // parts
    moved = lax.all_to_all(flat.reshape(parts, rows // fold, fold, LANE), axis, 0, 0, tiled=True)
    return moved.reshape(flat.shape)


def pack_kernel(x_ref, out_ref, src_ref, top_ref, *, parts, flip):
    step = pl.program_id(0)
    tile = x_ref.shape[0]
    width = tile // parts
    used = blocks_of(width, tile)
    rows = out_ref.shape[0] // parts
    x = x_ref[...]
    level = jnp.max(jnp.abs(x.astype(jnp.float32)), axis=0, keepdims=True)
    top_ref[...] = jnp.where(step == 0, level, jnp.maximum(top_ref[...], level))
    if flip:
        src_ref[pl.ds(pl.multiple_of(step * LANE, LANE), LANE), :] = x.astype(jnp.float32).T.astype(x.dtype)
    else:
        src_ref[:, pl.ds(pl.multiple_of(step * LANE, LANE), LANE)] = x

    @pl.when(step == pl.num_programs(0) - 1)
    def _():
        top = jnp.max(top_ref[...], axis=1, keepdims=True)
        foot = jnp.broadcast_to(top, (rows - used, LANE)).astype(out_ref.dtype)
        for t in range(parts):
            for block in range(tile // LANE):
                out_ref[t * rows + block * width : t * rows + (block + 1) * width, :] = src_ref[
                    t * width : (t + 1) * width, block * LANE : (block + 1) * LANE
                ]
            out_ref[t * rows + used : (t + 1) * rows, :] = foot


def pack(piece, parts, flip):
    tile = piece.shape[0]
    shape = (parts * (blocks_of(tile // parts, tile) + FOOT), LANE)
    return pl.pallas_call(
        lambda *refs: pack_kernel(*refs, parts=parts, flip=flip),
        grid=(tile // LANE,),
        out_shape=jax.ShapeDtypeStruct(shape, piece.dtype),
        in_specs=[pl.BlockSpec((tile, LANE), lambda i: (0, i))],
        out_specs=pl.BlockSpec(shape, lambda i: (0, 0)),
        scratch_shapes=[pltpu.VMEM((tile, tile), piece.dtype), pltpu.VMEM((1, LANE), jnp.float32)],
        compiler_params=pltpu.CompilerParams(vmem_limit_bytes=ROOM),
        name="pack_flip" if flip else "pack",
    )(pltpu.with_memory_space_constraint(piece, pltpu.HBM))


def mix_kernel(places, cap, in_ref, bank_hbm, out_ref, scale_ref, x_ref, prod_ref, bank_ref, sems):
    banks, tile, _ = bank_ref.shape
    lanes = x_ref.shape[0]
    parts = lanes // PAD
    width = tile // parts
    used = blocks_of(width, tile)
    rows = used + FOOT
    edges = [0, PAIR, banks // 2, banks]
    copies = {
        low: pltpu.make_async_copy(bank_hbm.at[pl.ds(low, high - low)], bank_ref.at[pl.ds(low, high - low)], sems.at[i])
        for i, (low, high) in enumerate(zip(edges[:-1], edges[1:]))
    }
    for copy in copies.values():
        copy.start()

    x_ref[...] = jnp.zeros(x_ref.shape, x_ref.dtype)

    top = jnp.zeros((1, LANE), jnp.float32)
    for t in range(parts):
        for block in range(tile // LANE):
            x_ref[t * PAD : t * PAD + width, block * LANE : (block + 1) * LANE] = in_ref[
                t * rows + block * width : t * rows + (block + 1) * width, :
            ]
        foot = in_ref[t * rows + used : (t + 1) * rows, :].astype(jnp.float32)
        top = jnp.maximum(top, foot[:1])
    scale = 32768.0 / jnp.maximum(top * cap[0], 1e-30)
    scale_ref[...] = 1.0 / scale
    prod_ref[pl.ds(banks * lanes, PAD), :] = jnp.zeros((PAD, tile), jnp.float32)

    for b in range(0, banks, PAIR):
        if b in copies:
            copies[b].wait()
        both = lax.dot_general(
            x_ref[...],
            bank_ref[b : b + PAIR].reshape(PAIR * tile, tile),
            (((1,), (1,)), ((), ())),
            preferred_element_type=jnp.float32,
        )
        for side in range(PAIR):
            prod_ref[pl.ds((b + side) * lanes, lanes), :] = both[:, side * tile : (side + 1) * tile]

    def gather(pair, carry):
        out = out_ref.at[pl.ds(pl.multiple_of(pair * (PAIR * used), PAIR * used), PAIR * used), :]
        for side in range(PAIR):
            totals = [None] * CHAINS
            for slot in range(places.shape[1]):
                piece = prod_ref[pl.ds(pl.multiple_of(places[pair * PAIR + side, slot], PAD), PAD), :]
                chain = slot % CHAINS
                totals[chain] = piece if totals[chain] is None else totals[chain] + piece
            total = sum(totals[1:], totals[0])
            for block in range(tile // LANE):
                out[side * used + block * width : side * used + (block + 1) * width, :] = (
                    total[:width, block * LANE : (block + 1) * LANE] * scale
                )
        return carry

    lax.fori_loop(0, parts // PAIR, gather, 0)


def mix(pieces, bank, places, cap):
    parts = places.shape[0]
    banks, tile, _ = bank.shape
    out, unscale = pl.pallas_call(
        mix_kernel,
        out_shape=(
            jax.ShapeDtypeStruct((parts * blocks_of(tile // parts, tile), LANE), jnp.float32),
            jax.ShapeDtypeStruct((1, LANE), jnp.float32),
        ),
        in_specs=[SMEM, SMEM, VMEM, pl.BlockSpec(memory_space=pltpu.HBM)],
        out_specs=(VMEM, VMEM),
        scratch_shapes=[
            pltpu.VMEM((parts * PAD, tile), pieces.dtype),
            pltpu.VMEM((banks * parts * PAD + PAD, tile), jnp.float32),
            pltpu.VMEM(bank.shape, bank.dtype),
            pltpu.SemaphoreType.DMA((3,)),
        ],
        compiler_params=pltpu.CompilerParams(vmem_limit_bytes=ROOM),
        name="mix",
    )(places, cap, inside(pieces), pltpu.with_memory_space_constraint(bank, pltpu.HBM))
    return out.astype(jnp.float16), unscale


def find(tiles, blocks, count, banks):
    rows, slots = tiles.shape
    at = blocks * (rows * PAD) + tiles * PAD
    return jnp.where(jnp.arange(slots) < count[:, None], at, banks * rows * PAD)


def piece_of(parts_ref, t, block, width, used):
    return parts_ref[t * used + block * width : t * used + (block + 1) * width, :]


def turn_kernel(parts_ref, unit, out_ref, flip_ref, *, parts):
    tile = out_ref.shape[0]
    width = tile // parts
    for t in range(parts):
        for block in range(tile // LANE):
            flip_ref[t * width : (t + 1) * width, block * LANE : (block + 1) * LANE] = piece_of(
                parts_ref, t, block, width, blocks_of(width, tile)
            )
    out_ref[...] = flip_ref[...].T * unit[0, 0]


def turn(flat, unit, parts, tile):
    return pl.pallas_call(
        lambda *refs: turn_kernel(*refs, parts=parts),
        out_shape=jax.ShapeDtypeStruct((tile, tile), jnp.float32),
        in_specs=[VMEM, SMEM],
        out_specs=VMEM,
        scratch_shapes=[pltpu.VMEM((tile, tile), jnp.float32)],
        compiler_params=pltpu.CompilerParams(vmem_limit_bytes=ROOM),
        name="turn",
    )(inside(flat.astype(jnp.float32)), unit)


def join_kernel(base_ref, parts_ref, unit, out_ref, *, parts):
    tile = out_ref.shape[0]
    width = tile // parts
    for t in range(parts):
        for block in range(tile // LANE):
            rows, cols = slice(t * width, (t + 1) * width), slice(block * LANE, (block + 1) * LANE)
            piece = piece_of(parts_ref, t, block, width, blocks_of(width, tile))
            out_ref[rows, cols] = base_ref[rows, cols] + piece * unit[0, 0]


def join(base, flat, unit, parts):
    return pl.pallas_call(
        lambda *refs: join_kernel(*refs, parts=parts),
        out_shape=jax.ShapeDtypeStruct(base.shape, jnp.float32),
        in_specs=[VMEM, VMEM, SMEM],
        out_specs=VMEM,
        compiler_params=pltpu.CompilerParams(vmem_limit_bytes=ROOM, allow_input_fusion=[False, True, False]),
        name="join",
    )(inside(base), flat.astype(jnp.float32), unit)


def local(coeff, bank, alpha_tiles, alpha_blocks, alpha_count, beta_tiles, beta_blocks, beta_count):
    tile = coeff.shape[0]
    banks = bank.shape[0]
    n_row = lax.axis_size("row")
    n_col = lax.axis_size("col")
    slots = alpha_tiles.shape[1]
    alpha_in = ship(pack(coeff, n_row, True), n_row, "row", FOOT)
    beta_in = ship(pack(coeff, n_col, False), n_col, "col", FOOT)
    cap = (jnp.max(jnp.abs(bank)).astype(jnp.float32) * (slots * tile)).reshape(1)
    alpha_at = find(alpha_tiles, alpha_blocks, alpha_count, banks)
    beta_at = find(beta_tiles, beta_blocks, beta_count, banks)
    alpha_mix, alpha_unit = mix(alpha_in, bank, alpha_at, cap)
    beta_mix, beta_unit = mix(beta_in, bank, beta_at, cap)
    alpha_out = ship(alpha_mix, n_row, "row", 2 * FOOT)
    beta_out = ship(beta_mix, n_col, "col", 2 * FOOT)
    base = turn(alpha_out, alpha_unit, n_row, tile)
    return join(base, beta_out, beta_unit, n_col)


def solution(mesh):
    return jax.shard_map(
        local,
        mesh=mesh,
        in_specs=(P("row", "col"), P(), P(), P(), P(), P(), P(), P()),
        out_specs=P("row", "col"),
        check_vma=False,
    )
```

profile of v0, /device:TPU:73, one launch (start us, length us, event | category | flops | bytes accessed | tf_op | source)
XLA Modules:
  0.0 121.5 jit_solution(9588335566640930813)
XLA Ops:
  0.0 2.8 %pack_flip.1 = bf16[1216,128]{1,0:T(8,128)(2,1)} custom-call(bf16[384,384]{1,0:T(8,128)(2,1)} %refs_0_.3), custom_call_target="tpu_custom_call" | custom-call | tf_op jit(solution)/shard_map/pack_flip/pallas_call | solution.py:61
  2.8 11.7 %all-to-all-start = ((bf16[32,19,2,128]{3,2,1,0:T(2,128)(2,1)}), bf16[32,19,2,128]{3,2,1,0:T(2,128)(2,1)S(1)}, u32[]{:S(2)}, u32[]{:S(2)}) async-start(bf16[32,19,2,128]{3,2,1,0:T(2,128)(2,1)} %bitcast.1), calls=%async_computation | async-start | bytes 622592 | tf_op jit(solution)/shard_map/all_to_all | solution.py:28
  14.5 2.7 %pack.1 = bf16[1216,128]{1,0:T(8,128)(2,1)} custom-call(bf16[384,384]{1,0:T(8,128)(2,1)} %refs_0_.3), custom_call_target="tpu_custom_call" | custom-call | tf_op jit(solution)/shard_map/pack/pallas_call | solution.py:61
  17.2 6.6 %all-to-all-done = bf16[32,19,2,128]{3,2,1,0:T(2,128)(2,1)S(1)} async-done(((bf16[32,19,2,128]{3,2,1,0:T(2,128)(2,1)}), bf16[32,19,2,128]{3,2,1,0:T(2,128)(2,1)S(1)}, u32[]{:S(2)}, u32[]{:S(2)}) %all-to-all-start) | async-done | bytes 311328 | tf_op jit(solution)/shard_map/all_to_all | solution.py:28
  23.8 22.8 %all-to-all-start.2 = ((bf16[32,19,2,128]{3,2,1,0:T(2,128)(2,1)}), bf16[32,19,2,128]{3,2,1,0:T(2,128)(2,1)S(1)}, u32[]{:S(2)}, u32[]{:S(2)}) async-start(bf16[32,19,2,128]{3,2,1,0:T(2,128)(2,1)} %bitcast.5), calls=%async_computation.2 | async-start | bytes 622592 | tf_op jit(solution)/shard_map/all_to_all | solution.py:28
  46.7 0.8 copy.10
  47.5 0.8 copy.9
  48.3 3.6 %abs_reduce_fusion = bf16[]{:T(256)} fusion(bf16[16,384,384]{2,1,0:T(8,128)(2,1)} %bank_hbm.3), kind=kLoop, calls=%fused_computation | loop fusion | flops 4718591 | bytes 4718594 | tf_op jit(solution)/shard_map/reduce_max | solution.py:217
  52.5 0.1 add_select_fusion.1.places
  52.6 7.2 %mix.2 = (f32[1152,128]{1,0:T(8,128)S(1)}, f32[1,128]{1,0:T(1,128)S(1)}) custom-call(s32[32,24]{1,0:T(8,128)S(1)} %add_select_fusion.1.places, f32[1]{0:T(128)} %bitcast.cap, bf16[1216,128]{1,0:T(8,128)(2,1)S(1)} %bitcast.12, bf16[16,384,384]{2,1,0:T(8,128)(2,1)} %bank_hbm.3), custom_call_target="tpu_custom_call" | custom-call | tf_op jit(solution)/shard_map/mix/pallas_call | solution.py:135
  59.7 0.8 convert_element_type.20
  60.5 12.4 %all-to-all-done.2 = bf16[32,19,2,128]{3,2,1,0:T(2,128)(2,1)S(1)} async-done(((bf16[32,19,2,128]{3,2,1,0:T(2,128)(2,1)}), bf16[32,19,2,128]{3,2,1,0:T(2,128)(2,1)S(1)}, u32[]{:S(2)}, u32[]{:S(2)}) %all-to-all-start.2) | async-done | bytes 311328 | tf_op jit(solution)/shard_map/all_to_all | solution.py:28
  72.9 4.0 %all-to-all-start.1 = ((f16[32,9,4,128]{3,2,1,0:T(4,128)(2,1)}), f16[32,9,4,128]{3,2,1,0:T(4,128)(2,1)S(1)}, u32[]{:S(2)}, u32[]{:S(2)}) async-start(f16[32,9,4,128]{3,2,1,0:T(4,128)(2,1)} %bitcast.3), calls=%async_computation.1 | async-start | bytes 589824 | tf_op jit(solution)/shard_map/all_to_all | solution.py:28
  76.9 0.1 copy.11
  77.0 0.1 copy.12
  77.1 0.0 copy-done.3
  77.1 0.1 add_select_fusion.places
  77.1 7.2 %mix.3 = (f32[1152,128]{1,0:T(8,128)S(1)}, f32[1,128]{1,0:T(1,128)S(1)}) custom-call(s32[32,24]{1,0:T(8,128)S(1)} %add_select_fusion.places, f32[1]{0:T(128)} %bitcast.cap, bf16[1216,128]{1,0:T(8,128)(2,1)S(1)} %bitcast.11, bf16[16,384,384]{2,1,0:T(8,128)(2,1)} %bank_hbm.3), custom_call_target="tpu_custom_call" | custom-call | tf_op jit(solution)/shard_map/mix/pallas_call | solution.py:135
  84.3 0.7 convert_element_type.23
  85.0 2.1 %all-to-all-done.1 = f16[32,9,4,128]{3,2,1,0:T(4,128)(2,1)S(1)} async-done(((f16[32,9,4,128]{3,2,1,0:T(4,128)(2,1)}), f16[32,9,4,128]{3,2,1,0:T(4,128)(2,1)S(1)}, u32[]{:S(2)}, u32[]{:S(2)}) %all-to-all-start.1) | async-done | bytes 294944 | tf_op jit(solution)/shard_map/all_to_all | solution.py:28
  87.2 6.4 %all-to-all-start.3 = ((f16[32,9,4,128]{3,2,1,0:T(4,128)(2,1)}), f16[32,9,4,128]{3,2,1,0:T(4,128)(2,1)S(1)}, u32[]{:S(2)}, u32[]{:S(2)}) async-start(f16[32,9,4,128]{3,2,1,0:T(4,128)(2,1)} %bitcast.7), calls=%async_computation.3 | async-start | bytes 589824 | tf_op jit(solution)/shard_map/all_to_all | solution.py:28
  93.6 25.6 %all-to-all-done.3 = f16[32,9,4,128]{3,2,1,0:T(4,128)(2,1)S(1)} async-done(((f16[32,9,4,128]{3,2,1,0:T(4,128)(2,1)}), f16[32,9,4,128]{3,2,1,0:T(4,128)(2,1)S(1)}, u32[]{:S(2)}, u32[]{:S(2)}) %all-to-all-start.3) | async-done | bytes 294944 | tf_op jit(solution)/shard_map/all_to_all | solution.py:28
  119.3 0.8 turn.1.refs_0_
  120.1 1.4 %join.1 = f32[384,384]{1,0:T(8,128)} custom-call(f32[384,384]{1,0:T(8,128)S(1)} %turn.1.refs_0_, f32[1152,128]{1,0:T(8,128)S(1)} %convert.3.refs_1_, f32[1,128]{1,0:T(1,128)S(1)} %get-tuple-element.12.refs_2_), custom_call_target="tpu_custom_call" | custom-call | tf_op jit(solution)/shard_map/join/pallas_call | solution.py:199
  (9 shorter events, 0.1 us)
Async XLA Ops:
  0.0 52.5 %copy-start.2 = (s32[32]{0:T(128)S(1)}, s32[32]{0:T(128)}, u32[]{:S(2)}) copy-start(s32[32]{0:T(128)} %param.12) | copy-start | bytes 388
  2.8 21.0 %all-to-all-start = ((bf16[32,19,2,128]{3,2,1,0:T(2,128)(2,1)}), bf16[32,19,2,128]{3,2,1,0:T(2,128)(2,1)S(1)}, u32[]{:S(2)}, u32[]{:S(2)}) async-start(bf16[32,19,2,128]{3,2,1,0:T(2,128)(2,1)} %bitcast.1), calls=%async_computation | async-start | bytes 622592 | tf_op jit(solution)/shard_map/all_to_all | solution.py:28
  23.8 49.0 %all-to-all-start.2 = ((bf16[32,19,2,128]{3,2,1,0:T(2,128)(2,1)}), bf16[32,19,2,128]{3,2,1,0:T(2,128)(2,1)S(1)}, u32[]{:S(2)}, u32[]{:S(2)}) async-start(bf16[32,19,2,128]{3,2,1,0:T(2,128)(2,1)} %bitcast.5), calls=%async_computation.2 | async-start | bytes 622592 | tf_op jit(solution)/shard_map/all_to_all | solution.py:28
  48.2 28.7 %copy-start = (s32[32,24]{0,1:T(8,128)S(1)}, s32[32,24]{0,1:T(8,128)}, u32[]{:S(2)}) copy-start(s32[32,24]{0,1:T(8,128)} %param.14) | copy-start | bytes 9220
  48.2 28.7 %copy-start.1 = (s32[32,24]{0,1:T(8,128)S(1)}, s32[32,24]{0,1:T(8,128)}, u32[]{:S(2)}) copy-start(s32[32,24]{0,1:T(8,128)} %param.13) | copy-start | bytes 9220
  48.2 28.8 %copy-start.3 = (s32[32]{0:T(128)S(1)}, s32[32]{0:T(128)}, u32[]{:S(2)}) copy-start(s32[32]{0:T(128)} %param.15) | copy-start | bytes 388
  72.9 14.3 %all-to-all-start.1 = ((f16[32,9,4,128]{3,2,1,0:T(4,128)(2,1)}), f16[32,9,4,128]{3,2,1,0:T(4,128)(2,1)S(1)}, u32[]{:S(2)}, u32[]{:S(2)}) async-start(f16[32,9,4,128]{3,2,1,0:T(4,128)(2,1)} %bitcast.3), calls=%async_computation.1 | async-start | bytes 589824 | tf_op jit(solution)/shard_map/all_to_all | solution.py:28
  87.2 32.1 %all-to-all-start.3 = ((f16[32,9,4,128]{3,2,1,0:T(4,128)(2,1)}), f16[32,9,4,128]{3,2,1,0:T(4,128)(2,1)S(1)}, u32[]{:S(2)}, u32[]{:S(2)}) async-start(f16[32,9,4,128]{3,2,1,0:T(4,128)(2,1)} %bitcast.7), calls=%async_computation.3 | async-start | bytes 589824 | tf_op jit(solution)/shard_map/all_to_all | solution.py:28
where the time goes:
time: 122 us
  waiting for transfers between devices  46.8 us (38%)
  starting transfers between devices  44.9 us (37%)
  Pallas kernels  22.1 us (18%)
  other arithmetic  5.32 us (4%)
  local copies, waits for them, and re-layouts  1.72 us (1%)
    all_to_all x4, waiting for transfers between devices, ship(): lax.all_to_all(flat.reshape(parts, rows // fold, fold, LANE), axis, 0, 0,...  46.8 us
    all_to_all x4, starting transfers between devices, ship(): lax.all_to_all(flat.reshape(parts, rows // fold, fold, LANE), axis, 0, 0,...  44.9 us
    pallas_call x2, Pallas kernels, mix(): pl.pallas_call(mix_kernel, out_shape=(jax.ShapeDtypeStruct((parts * block...  14.3 us
    pallas_call x2, Pallas kernels, pack(): pl.pallas_call(lambda *refs: pack_kernel(*refs, parts=parts, flip=flip),...  5.53 us
    reduce_max x1, other arithmetic, local(): jnp.max(jnp.abs(bank)).astype(jnp.float32) * (slots * tile)  3.59 us
  transfers between devices with their start and end apart: 4, of which 4 were waited for; matrix products, arithmetic and copies ran while one was open for 6% of the time, Pallas kernels for 14%

commit v1 on v0

--- a/solution.py
+++ b/solution.py
@@ -29,45 +29,38 @@
     return moved.reshape(flat.shape)
 
 
-def pack_kernel(x_ref, out_ref, src_ref, top_ref, *, parts, flip):
-    step = pl.program_id(0)
+def pack_kernel(x_ref, out_ref, flip_ref, *, parts, flip):
     tile = x_ref.shape[0]
     width = tile // parts
     used = blocks_of(width, tile)
     rows = out_ref.shape[0] // parts
     x = x_ref[...]
-    level = jnp.max(jnp.abs(x.astype(jnp.float32)), axis=0, keepdims=True)
-    top_ref[...] = jnp.where(step == 0, level, jnp.maximum(top_ref[...], level))
+    top = jnp.max(jnp.max(jnp.abs(x.astype(jnp.float32)), axis=0, keepdims=True), axis=1, keepdims=True)
+    foot = jnp.broadcast_to(top, (rows - used, LANE)).astype(out_ref.dtype)
     if flip:
-        src_ref[pl.ds(pl.multiple_of(step * LANE, LANE), LANE), :] = x.astype(jnp.float32).T.astype(x.dtype)
+        flip_ref[...] = x.astype(jnp.float32).T.astype(x.dtype)
+        src = flip_ref
     else:
-        src_ref[:, pl.ds(pl.multiple_of(step * LANE, LANE), LANE)] = x
-
-    @pl.when(step == pl.num_programs(0) - 1)
-    def _():
-        top = jnp.max(top_ref[...], axis=1, keepdims=True)
-        foot = jnp.broadcast_to(top, (rows - used, LANE)).astype(out_ref.dtype)
-        for t in range(parts):
-            for block in range(tile // LANE):
-                out_ref[t * rows + block * width : t * rows + (block + 1) * width, :] = src_ref[
-                    t * width : (t + 1) * width, block * LANE : (block + 1) * LANE
-                ]
-            out_ref[t * rows + used : (t + 1) * rows, :] = foot
+        src = x_ref
+    for t in range(parts):
+        for block in range(tile // LANE):
+            out_ref[t * rows + block * width : t * rows + (block + 1) * width, :] = src[
+                t * width : (t + 1) * width, block * LANE : (block + 1) * LANE
+            ]
+        out_ref[t * rows + used : (t + 1) * rows, :] = foot
 
 
 def pack(piece, parts, flip):
     tile = piece.shape[0]
-    shape = (parts * (blocks_of(tile // parts, tile) + FOOT), LANE)
     return pl.pallas_call(
         lambda *refs: pack_kernel(*refs, parts=parts, flip=flip),
-        grid=(tile // LANE,),
-        out_shape=jax.ShapeDtypeStruct(shape, piece.dtype),
-        in_specs=[pl.BlockSpec((tile, LANE), lambda i: (0, i))],
-        out_specs=pl.BlockSpec(shape, lambda i: (0, 0)),
-        scratch_shapes=[pltpu.VMEM((tile, tile), piece.dtype), pltpu.VMEM((1, LANE), jnp.float32)],
+        out_shape=jax.ShapeDtypeStruct((parts * (blocks_of(tile // parts, tile) + FOOT), LANE), piece.dtype),
+        in_specs=[VMEM],
+        out_specs=VMEM,
+        scratch_shapes=[pltpu.VMEM((tile, tile), piece.dtype)],
         compiler_params=pltpu.CompilerParams(vmem_limit_bytes=ROOM),
         name="pack_flip" if flip else "pack",
-    )(pltpu.with_memory_space_constraint(piece, pltpu.HBM))
+    )(piece)
 
 
 def mix_kernel(places, cap, in_ref, bank_hbm, out_ref, scale_ref, x_ref, prod_ref, bank_ref, sems):

time: 122 us -> 121 us (level)
  Pallas kernels: 22.1 us -> 18.4 us
  local copies, waits for them, and re-layouts: 1.72 us -> 3.64 us
    pallas_call x2, Pallas kernels: 5.53 us -> 1.84 us  [pack(): pl.pallas_call(lambda *refs: pack_kernel(*refs, parts=parts, flip=flip),...]
    unnamed x12 -> x16, local copies, waits for them, and re-layouts: 1.72 us -> 3.64 us
  transfers between devices with their start and end apart: 4 -> 4, of which waited for: 4 -> 4; matrix products, arithmetic and copies ran while one was open for 6% -> 6% of each run, Pallas kernels for 14% -> 13%
where the time goes in v1:
time: 121 us
  waiting for transfers between devices  47.6 us (39%)
  starting transfers between devices  44.9 us (37%)
  Pallas kernels  18.4 us (15%)
  other arithmetic  5.33 us (4%)
  local copies, waits for them, and re-layouts  3.64 us (3%)
    all_to_all x4, waiting for transfers between devices, ship(): lax.all_to_all(flat.reshape(parts, rows // fold, fold, LANE), axis, 0, 0,...  47.6 us
    all_to_all x4, starting transfers between devices, ship(): lax.all_to_all(flat.reshape(parts, rows // fold, fold, LANE), axis, 0, 0,...  44.9 us
    pallas_call x2, Pallas kernels, mix(): pl.pallas_call(mix_kernel, out_shape=(jax.ShapeDtypeStruct((parts * block...  14.3 us
    unnamed x16, local copies, waits for them, and re-layouts  3.64 us
    reduce_max x1, other arithmetic, local(): jnp.max(jnp.abs(bank)).astype(jnp.float32) * (slots * tile)  3.59 us
  transfers between devices with their start and end apart: 4, of which 4 were waited for; matrix products, arithmetic and copies ran while one was open for 6% of the time, Pallas kernels for 13%

profile of v1, /device:TPU:73, one launch (start us, length us, event | category | flops | bytes accessed | tf_op | source)
XLA Modules:
  0.0 120.6 jit_solution(9446947586628432337)
XLA Ops:
  0.0 1.0 copy-done
  1.0 1.0 pack_flip.1
  2.0 11.7 %all-to-all-start = ((bf16[32,19,2,128]{3,2,1,0:T(2,128)(2,1)}), bf16[32,19,2,128]{3,2,1,0:T(2,128)(2,1)S(1)}, u32[]{:S(2)}, u32[]{:S(2)}) async-start(bf16[32,19,2,128]{3,2,1,0:T(2,128)(2,1)} %bitcast.1), calls=%async_computation | async-start | bytes 622592 | tf_op jit(solution)/shard_map/all_to_all | solution.py:28
  13.6 1.0 copy-done.1
  14.6 0.8 pack.1
  15.4 7.5 %all-to-all-done = bf16[32,19,2,128]{3,2,1,0:T(2,128)(2,1)S(1)} async-done(((bf16[32,19,2,128]{3,2,1,0:T(2,128)(2,1)}), bf16[32,19,2,128]{3,2,1,0:T(2,128)(2,1)S(1)}, u32[]{:S(2)}, u32[]{:S(2)}) %all-to-all-start) | async-done | bytes 311328 | tf_op jit(solution)/shard_map/all_to_all | solution.py:28
  23.0 22.8 %all-to-all-start.2 = ((bf16[32,19,2,128]{3,2,1,0:T(2,128)(2,1)}), bf16[32,19,2,128]{3,2,1,0:T(2,128)(2,1)S(1)}, u32[]{:S(2)}, u32[]{:S(2)}) async-start(bf16[32,19,2,128]{3,2,1,0:T(2,128)(2,1)} %bitcast.5), calls=%async_computation.2 | async-start | bytes 622592 | tf_op jit(solution)/shard_map/all_to_all | solution.py:28
  45.8 0.8 copy.10
  46.6 0.8 copy.9
  47.4 3.6 %abs_reduce_fusion = bf16[]{:T(256)} fusion(bf16[16,384,384]{2,1,0:T(8,128)(2,1)} %bank_hbm.3), kind=kLoop, calls=%fused_computation | loop fusion | flops 4718591 | bytes 4718594 | tf_op jit(solution)/shard_map/reduce_max | solution.py:210
  51.6 0.1 add_select_fusion.1.places
  51.7 7.1 %mix.2 = (f32[1152,128]{1,0:T(8,128)S(1)}, f32[1,128]{1,0:T(1,128)S(1)}) custom-call(s32[32,24]{1,0:T(8,128)S(1)} %add_select_fusion.1.places, f32[1]{0:T(128)} %bitcast.cap, bf16[1216,128]{1,0:T(8,128)(2,1)S(1)} %bitcast.12, bf16[16,384,384]{2,1,0:T(8,128)(2,1)} %bank_hbm.3), custom_call_target="tpu_custom_call" | custom-call | tf_op jit(solution)/shard_map/mix/pallas_call | solution.py:128
  58.9 0.8 convert_element_type.20
  59.6 12.4 %all-to-all-done.2 = bf16[32,19,2,128]{3,2,1,0:T(2,128)(2,1)S(1)} async-done(((bf16[32,19,2,128]{3,2,1,0:T(2,128)(2,1)}), bf16[32,19,2,128]{3,2,1,0:T(2,128)(2,1)S(1)}, u32[]{:S(2)}, u32[]{:S(2)}) %all-to-all-start.2) | async-done | bytes 311328 | tf_op jit(solution)/shard_map/all_to_all | solution.py:28
  72.0 4.0 %all-to-all-start.1 = ((f16[32,9,4,128]{3,2,1,0:T(4,128)(2,1)}), f16[32,9,4,128]{3,2,1,0:T(4,128)(2,1)S(1)}, u32[]{:S(2)}, u32[]{:S(2)}) async-start(f16[32,9,4,128]{3,2,1,0:T(4,128)(2,1)} %bitcast.3), calls=%async_computation.1 | async-start | bytes 589824 | tf_op jit(solution)/shard_map/all_to_all | solution.py:28
  76.0 0.1 copy.11
  76.2 0.1 add_select_fusion.places
  76.2 7.2 %mix.3 = (f32[1152,128]{1,0:T(8,128)S(1)}, f32[1,128]{1,0:T(1,128)S(1)}) custom-call(s32[32,24]{1,0:T(8,128)S(1)} %add_select_fusion.places, f32[1]{0:T(128)} %bitcast.cap, bf16[1216,128]{1,0:T(8,128)(2,1)S(1)} %bitcast.11, bf16[16,384,384]{2,1,0:T(8,128)(2,1)} %bank_hbm.3), custom_call_target="tpu_custom_call" | custom-call | tf_op jit(solution)/shard_map/mix/pallas_call | solution.py:128
  83.4 0.8 convert_element_type.23
  84.2 2.1 %all-to-all-done.1 = f16[32,9,4,128]{3,2,1,0:T(4,128)(2,1)S(1)} async-done(((f16[32,9,4,128]{3,2,1,0:T(4,128)(2,1)}), f16[32,9,4,128]{3,2,1,0:T(4,128)(2,1)S(1)}, u32[]{:S(2)}, u32[]{:S(2)}) %all-to-all-start.1) | async-done | bytes 294944 | tf_op jit(solution)/shard_map/all_to_all | solution.py:28
  86.3 6.4 %all-to-all-start.3 = ((f16[32,9,4,128]{3,2,1,0:T(4,128)(2,1)}), f16[32,9,4,128]{3,2,1,0:T(4,128)(2,1)S(1)}, u32[]{:S(2)}, u32[]{:S(2)}) async-start(f16[32,9,4,128]{3,2,1,0:T(4,128)(2,1)} %bitcast.7), calls=%async_computation.3 | async-start | bytes 589824 | tf_op jit(solution)/shard_map/all_to_all | solution.py:28
  92.7 25.6 %all-to-all-done.3 = f16[32,9,4,128]{3,2,1,0:T(4,128)(2,1)S(1)} async-done(((f16[32,9,4,128]{3,2,1,0:T(4,128)(2,1)}), f16[32,9,4,128]{3,2,1,0:T(4,128)(2,1)S(1)}, u32[]{:S(2)}, u32[]{:S(2)}) %all-to-all-start.3) | async-done | bytes 294944 | tf_op jit(solution)/shard_map/all_to_all | solution.py:28
  118.4 0.8 turn.1.refs_0_
  119.2 1.4 %join.1 = f32[384,384]{1,0:T(8,128)} custom-call(f32[384,384]{1,0:T(8,128)S(1)} %turn.1.refs_0_, f32[1152,128]{1,0:T(8,128)S(1)} %convert.3.refs_1_, f32[1,128]{1,0:T(1,128)S(1)} %get-tuple-element.12.refs_2_), custom_call_target="tpu_custom_call" | custom-call | tf_op jit(solution)/shard_map/join/pallas_call | solution.py:192
  (13 shorter events, 0.2 us)
Async XLA Ops:
  0.0 1.0 copy-start
  1.0 50.7 %copy-start.4 = (s32[32]{0:T(128)S(1)}, s32[32]{0:T(128)}, u32[]{:S(2)}) copy-start(s32[32]{0:T(128)} %param.12) | copy-start | bytes 388
  2.0 21.0 %all-to-all-start = ((bf16[32,19,2,128]{3,2,1,0:T(2,128)(2,1)}), bf16[32,19,2,128]{3,2,1,0:T(2,128)(2,1)S(1)}, u32[]{:S(2)}, u32[]{:S(2)}) async-start(bf16[32,19,2,128]{3,2,1,0:T(2,128)(2,1)} %bitcast.1), calls=%async_computation | async-start | bytes 622592 | tf_op jit(solution)/shard_map/all_to_all | solution.py:28
  13.6 1.0 copy-start.1
  23.0 49.0 %all-to-all-start.2 = ((bf16[32,19,2,128]{3,2,1,0:T(2,128)(2,1)}), bf16[32,19,2,128]{3,2,1,0:T(2,128)(2,1)S(1)}, u32[]{:S(2)}, u32[]{:S(2)}) async-start(bf16[32,19,2,128]{3,2,1,0:T(2,128)(2,1)} %bitcast.5), calls=%async_computation.2 | async-start | bytes 622592 | tf_op jit(solution)/shard_map/all_to_all | solution.py:28
  47.4 28.7 %copy-start.2 = (s32[32,24]{0,1:T(8,128)S(1)}, s32[32,24]{0,1:T(8,128)}, u32[]{:S(2)}) copy-start(s32[32,24]{0,1:T(8,128)} %param.14) | copy-start | bytes 9220
  47.4 28.7 %copy-start.3 = (s32[32,24]{0,1:T(8,128)S(1)}, s32[32,24]{0,1:T(8,128)}, u32[]{:S(2)}) copy-start(s32[32,24]{0,1:T(8,128)} %param.13) | copy-start | bytes 9220
  47.4 28.8 %copy-start.5 = (s32[32]{0:T(128)S(1)}, s32[32]{0:T(128)}, u32[]{:S(2)}) copy-start(s32[32]{0:T(128)} %param.15) | copy-start | bytes 388
  72.0 14.3 %all-to-all-start.1 = ((f16[32,9,4,128]{3,2,1,0:T(4,128)(2,1)}), f16[32,9,4,128]{3,2,1,0:T(4,128)(2,1)S(1)}, u32[]{:S(2)}, u32[]{:S(2)}) async-start(f16[32,9,4,128]{3,2,1,0:T(4,128)(2,1)} %bitcast.3), calls=%async_computation.1 | async-start | bytes 589824 | tf_op jit(solution)/shard_map/all_to_all | solution.py:28
  86.3 32.1 %all-to-all-start.3 = ((f16[32,9,4,128]{3,2,1,0:T(4,128)(2,1)}), f16[32,9,4,128]{3,2,1,0:T(4,128)(2,1)S(1)}, u32[]{:S(2)}, u32[]{:S(2)}) async-start(f16[32,9,4,128]{3,2,1,0:T(4,128)(2,1)} %bitcast.7), calls=%async_computation.3 | async-start | bytes 589824 | tf_op jit(solution)/shard_map/all_to_all | solution.py:28
